TPU v7x, 256 devices: a whole 4x4x8 slice. The times are simulated.
256 devices in a mesh: span: 32 (over z, y_hi, core), head: 8 (over x, y_lo).
Axes of the slice: x: 4, y: 4 (y_hi: 2, y_lo: 2; y = y_hi * 2 + y_lo), z: 8, core: 2. Of those that a mesh axis runs over, the one named last changes fastest.
Arguments:
- queries: bfloat16 [16384, 6144], P('span', 'head'), may hold values from -16 to 16
- stacked_key_vectors: bfloat16 [16384, 1024], P('span', 'head'), may hold values from -16 to 16
- stacked_value_vectors: bfloat16 [16384, 1024], P('span', 'head'), may hold values from -6 to 6
- out_weight: bfloat16 [6144, 6144], P('head'), may hold values from -0.625 to 0.625
- residual: bfloat16 [16384, 6144], P(('span', 'head')), may hold values from -6 to 6
- gate_table: float32 [32, 6144], replicated, may hold values from 0.25 to 1.75
- noise_step: int32 [32], replicated, may hold values from 0 to 31
- older_count: int32 [32], replicated, may hold values from 0 to 7, as said below
Outputs:
- output: bfloat16 [16384, 6144], P(('span', 'head'))
Inputs may be any that keep to these rules, and one draw needn't show every extreme that they name: older_count[c] is at most c; some span has exactly 7.
All inputs are finite; a program needn't handle non-finite values.
Results may differ from a plain program's by a relative error of at most 0.014.
Values may be sent and summed in bfloat16 or wider, within the bound.
A program may use at most 64 MiB of HBM per device.

v0:
```python
import math

import jax
import jax.numpy as jnp
from jax import lax
from jax.sharding import PartitionSpec as P

HEAD_SIZE = 128
OLDER_SPAN_LIMIT = 7


def shifted(block, axis, distance):
    devices = range(lax.axis_size(axis))
    route = [(i - distance, i) for i in devices if i - distance in devices]
    return lax.ppermute(block, axis, route)


def on_device(
    queries,
    stacked_key_vectors,
    stacked_value_vectors,
    out_weight,
    residual,
    gate_table,
    noise_step,
    older_count,
):
    span_len = queries.shape[0]
    kv_heads = stacked_key_vectors.shape[1] // HEAD_SIZE
    q_heads = queries.shape[1] // HEAD_SIZE
    query_group_size = q_heads // kv_heads
    my_span = lax.axis_index("span")
    older_mine = older_count[my_span]
    grouped = queries.reshape(span_len, kv_heads, query_group_size, HEAD_SIZE)
    kv_pair = jnp.stack([stacked_key_vectors, stacked_value_vectors])
    score_scale = 1.0 / math.sqrt(HEAD_SIZE)

    def update(carry_state, kv_block):
        running_max, row_total, weighted = carry_state
        key_row_block = kv_block[0].reshape(kv_block.shape[1], kv_heads, HEAD_SIZE)
        value_row_block = kv_block[1].reshape(kv_block.shape[1], kv_heads, HEAD_SIZE)
        scores = (
            jnp.einsum("tgrd,ugd->grtu", grouped, key_row_block, preferred_element_type=jnp.float32)
            * score_scale
        )
        new_max = jnp.maximum(running_max, jnp.max(scores, axis=-1))
        rescale = jnp.exp(running_max - new_max)
        weights = jnp.exp(scores - new_max[..., None])
        row_total = row_total * rescale + jnp.sum(weights, axis=-1)
        added = jnp.einsum(
            "grtu,ugd->grtd",
            weights.astype(jnp.bfloat16),
            value_row_block,
            preferred_element_type=jnp.float32,
        )
        weighted = weighted * rescale[..., None] + added
        return (new_max, row_total, weighted)

    def keep_state(carry_state):
        return carry_state

    initial = (
        jnp.full((kv_heads, query_group_size, span_len), -1e30, jnp.float32),
        jnp.zeros((kv_heads, query_group_size, span_len), jnp.float32),
        jnp.zeros((kv_heads, query_group_size, span_len, HEAD_SIZE), jnp.float32),
    )
    final_state = update(initial, kv_pair)
    moving = kv_pair
    for distance in range(1, OLDER_SPAN_LIMIT + 1):
        moving = shifted(moving, "span", 1)
        guarded_kv_block = moving
        visible = (distance >= 0) & (distance <= older_mine)
        final_state = lax.cond(
            visible, lambda current: update(current, guarded_kv_block), keep_state, final_state
        )
    running_max, row_total, weighted = final_state
    attention = (weighted / row_total[..., None]).astype(jnp.bfloat16)
    attention = attention.transpose(2, 0, 1, 3).reshape(span_len, q_heads * HEAD_SIZE)
    projected = lax.psum_scatter(
        jnp.dot(attention, out_weight, preferred_element_type=jnp.float32).astype(jnp.bfloat16),
        "head",
        scatter_dimension=0,
        tiled=True,
    ).astype(jnp.float32)
    step_mine = noise_step[my_span]
    one_hot = (jnp.arange(gate_table.shape[0], dtype=jnp.int32) == step_mine).astype(jnp.float32)
    gate_row = jnp.dot(one_hot[None, :], gate_table, precision=lax.Precision.HIGHEST)
    return (residual.astype(jnp.float32) + gate_row * projected).astype(jnp.bfloat16)


def solution(mesh):
    in_specs = (
        P("span", "head"),
        P("span", "head"),
        P("span", "head"),
        P("head", None),
        P(("span", "head"), None),
        P(),
        P(),
        P(),
    )
    out_specs = P(("span", "head"), None)
    return jax.shard_map(
        on_device, mesh=mesh, in_specs=in_specs, out_specs=out_specs, check_vma=False
    )
```

profile of v0, /device:TPU:160, one launch (start us, length us, event | category | flops | bytes accessed | tf_op | source)
XLA Modules:
  0.0 270.3 jit_solution(2742605595410144956)
XLA Ops:
  6.5 0.0 copy-start
  6.5 0.0 reduce-scatter.2.cloned.1.call-start
  6.5 1.1 pad_maximum_fusion
  7.6 1.9 collective-permute-start
  9.6 8.2 %collective-permute-done = bf16[2,512,128]{2,1,0:T(8,128)(2,1)S(1)} collective-permute-done((bf16[2,512,128]{2,1,0:T(8,128)(2,1)S(1)}, bf16[2,512,128]{2,1,0:T(8,128)(2,1)S(1)}, u32[]{:S(2)}, u32[]{:S(2)}) %collective-permute-start) | collective-permute-done | bytes 262176 | tf_op jit(solution)/shard_map/ppermute | solution.py:15
  17.7 1.9 collective-permute-start.1
  19.6 8.2 %collective-permute-done.1 = bf16[2,512,128]{2,1,0:T(8,128)(2,1)S(1)} collective-permute-done((bf16[2,512,128]{2,1,0:T(8,128)(2,1)S(1)}, bf16[2,512,128]{2,1,0:T(8,128)(2,1)S(1)}, u32[]{:S(2)}, u32[]{:S(2)}) %collective-permute-start.1) | collective-permute-done | bytes 262176 | tf_op jit(solution)/shard_map/ppermute | solution.py:15
  27.8 1.9 collective-permute-start.2
  29.7 8.2 %collective-permute-done.2 = bf16[2,512,128]{2,1,0:T(8,128)(2,1)S(1)} collective-permute-done((bf16[2,512,128]{2,1,0:T(8,128)(2,1)S(1)}, bf16[2,512,128]{2,1,0:T(8,128)(2,1)S(1)}, u32[]{:S(2)}, u32[]{:S(2)}) %collective-permute-start.2) | collective-permute-done | bytes 262176 | tf_op jit(solution)/shard_map/ppermute | solution.py:15
  37.9 1.9 collective-permute-start.3
  39.8 1.4 copy.25
  41.2 6.8 %collective-permute-done.3 = bf16[2,512,128]{2,1,0:T(8,128)(2,1)S(1)} collective-permute-done((bf16[2,512,128]{2,1,0:T(8,128)(2,1)S(1)}, bf16[2,512,128]{2,1,0:T(8,128)(2,1)S(1)}, u32[]{:S(2)}, u32[]{:S(2)}) %collective-permute-start.3) | collective-permute-done | bytes 262176 | tf_op jit(solution)/shard_map/ppermute | solution.py:15
  48.0 1.9 collective-permute-start.4
  49.9 1.9 bitcast_reduce_fusion.7
  51.8 6.3 %collective-permute-done.4 = bf16[2,512,128]{2,1,0:T(8,128)(2,1)S(1)} collective-permute-done((bf16[2,512,128]{2,1,0:T(8,128)(2,1)S(1)}, bf16[2,512,128]{2,1,0:T(8,128)(2,1)S(1)}, u32[]{:S(2)}, u32[]{:S(2)}) %collective-permute-start.4) | collective-permute-done | bytes 262176 | tf_op jit(solution)/shard_map/ppermute | solution.py:15
  58.1 1.9 collective-permute-start.5
  60.0 0.0 copy-start.13
  60.0 1.7 add_bitcast_fusion
  61.7 6.5 %collective-permute-done.5 = bf16[2,512,128]{2,1,0:T(8,128)(2,1)} collective-permute-done((bf16[2,512,128]{2,1,0:T(8,128)(2,1)S(1)}, bf16[2,512,128]{2,1,0:T(8,128)(2,1)}, u32[]{:S(2)}, u32[]{:S(2)}) %collective-permute-start.5) | collective-permute-done | bytes 262176 | tf_op jit(solution)/shard_map/ppermute | solution.py:15
  68.3 1.9 collective-permute-start.6
  70.2 1.0 fusion.129
  71.2 0.6 dynamic_slice.7
  76.2 4.9 %conditional.7 = ((f32[1,6,512]{2,1,0:T(8,128)S(1)}, f32[1,6,512]{2,1,0:T(8,128)S(1)}, f32[1,6,512,128]{3,2,1,0:T(8,128)S(1)})) conditional(s32[]{:T(128)} %bitcast.107, (f32[1,6,512]{2,1,0:T(8,128)S(1)}, f32[1,6,512]{2,1,0:T(8,128)S(1)}, f32[1,6,512,128]{3,2,1,0:T(8,128)S(1)}) %tuple.49, (bf16[2,512,128]{2,1,0:T(8,128)(2,1)}, ...), branch_computations={%region_2.0_spmd, %region_3.0_spmd} | conditional | flops 818684928 | bytes 24322108 | solution.py:73
  76.3 0.0 copy-start.12
  76.3 1.9 bitcast_reduce_fusion
  78.2 1.0 fusion.2
  79.3 1.8 bitcast_add_fusion
  81.1 4.9 %conditional.8 = ((f32[1,6,512]{2,1,0:T(8,128)S(1)}, f32[1,6,512]{2,1,0:T(8,128)S(1)}, f32[1,6,512,128]{3,2,1,0:T(8,128)S(1)})) conditional(s32[]{:T(128)} %bitcast.106, (f32[1,6,512]{2,1,0:T(8,128)S(1)}, f32[1,6,512]{2,1,0:T(8,128)S(1)}, f32[1,6,512,128]{3,2,1,0:T(8,128)S(1)}) %get-tuple-element.301, (bf16[2,512,128]{2,1,0:T(8,128)(2,1)}, ...), branch_computations={%region_6.0_spmd, %region_7.0_spmd} | conditional | flops 818684928 | bytes 24322108 | solution.py:73
  81.2 1.9 bitcast_reduce_fusion.1
  83.1 1.0 fusion.20
  84.2 1.8 bitcast_add_fusion.2
  86.0 5.1 %conditional.9 = ((f32[1,6,512]{2,1,0:T(8,128)S(1)}, f32[1,6,512]{2,1,0:T(8,128)S(1)}, f32[1,6,512,128]{3,2,1,0:T(8,128)S(1)})) conditional(s32[]{:T(128)} %bitcast.105, (f32[1,6,512]{2,1,0:T(8,128)S(1)}, f32[1,6,512]{2,1,0:T(8,128)S(1)}, f32[1,6,512,128]{3,2,1,0:T(8,128)S(1)}) %get-tuple-element.302, (bf16[2,512,128]{2,1,0:T(8,128)(2,1)}, ...), branch_computations={%region_10.0_spmd, %region_11.0_spmd} | conditional | flops 818684928 | bytes 24322108 | solution.py:73
  86.2 0.0 copy-start.8
  86.2 1.9 bitcast_reduce_fusion.2
  88.2 1.0 fusion.38
  89.3 1.8 bitcast_add_fusion.4
  91.1 4.9 %conditional.10 = ((f32[1,6,512]{2,1,0:T(8,128)S(1)}, f32[1,6,512]{2,1,0:T(8,128)S(1)}, f32[1,6,512,128]{3,2,1,0:T(8,128)S(1)})) conditional(s32[]{:T(128)} %bitcast.104, (f32[1,6,512]{2,1,0:T(8,128)S(1)}, f32[1,6,512]{2,1,0:T(8,128)S(1)}, f32[1,6,512,128]{3,2,1,0:T(8,128)S(1)}) %get-tuple-element.303, (bf16[2,512,128]{2,1,0:T(8,128)(2,1)}, ...), branch_computations={%region_14.0_spmd, %region_15.0_spmd} | conditional | flops 818684928 | bytes 24322108 | solution.py:73
  91.1 0.0 copy-start.6
  91.1 1.9 bitcast_reduce_fusion.3
  93.1 1.0 fusion.56
  94.2 1.8 bitcast_add_fusion.6
  96.0 4.9 %conditional.11 = ((f32[1,6,512]{2,1,0:T(8,128)S(1)}, f32[1,6,512]{2,1,0:T(8,128)S(1)}, f32[1,6,512,128]{3,2,1,0:T(8,128)S(1)})) conditional(s32[]{:T(128)} %bitcast.103, (f32[1,6,512]{2,1,0:T(8,128)S(1)}, f32[1,6,512]{2,1,0:T(8,128)S(1)}, f32[1,6,512,128]{3,2,1,0:T(8,128)S(1)}) %get-tuple-element.304, (bf16[2,512,128]{2,1,0:T(8,128)(2,1)}, ...), branch_computations={%region_18.0_spmd, %region_19.0_spmd} | conditional | flops 818684928 | bytes 24322108 | solution.py:73
  96.0 0.0 copy-start.4
  96.0 1.9 bitcast_reduce_fusion.4
  98.0 1.0 fusion.74
  99.1 1.8 bitcast_add_fusion.8
  100.9 5.9 %conditional.12 = ((f32[1,6,512]{2,1,0:T(8,128)S(1)}, f32[1,6,512]{2,1,0:T(8,128)S(1)}, f32[1,6,512,128]{3,2,1,0:T(8,128)S(1)})) conditional(s32[]{:T(128)} %bitcast.102, (f32[1,6,512]{2,1,0:T(8,128)S(1)}, f32[1,6,512]{2,1,0:T(8,128)S(1)}, f32[1,6,512,128]{3,2,1,0:T(8,128)S(1)}) %get-tuple-element.305, (bf16[2,512,128]{2,1,0:T(8,128)(2,1)}, ...), branch_computations={%region_22.0_spmd, %region_23.0_spmd} | conditional | flops 818684928 | bytes 23265312 | solution.py:73
  101.1 1.9 bitcast_reduce_fusion.5
  103.0 1.0 fusion.92
  104.1 2.7 %bitcast_add_fusion.10 = f32[1,6,512,128]{3,2,1,0:T(8,128)S(1)} fusion(f32[1,6,512,128]{3,2,1,0:T(8,128)S(1)} %get-tuple-element.144, f32[512,512,6]{1,0,2:T(8,128)S(1)} %get-tuple-element.255, f32[6,512]{1,0:T(8,128)S(1)} %bitcast.420, f32[6,512]{1,0:T(8,128)S(1)} %get-tuple-element.238, bf16[2,512,128]{2,1,0:T(8,128)(2,1)} %get-tuple-element.141), kind=kOutput, calls=%fused_computation.114 | convolution fusion | flops 408158208 | bytes 9592832 | tf_op jit(solution)/shard_map/cond/branch_1_fun/grtu,ugd->grtd/dot_general | solution.py:50
  106.8 0.0 collective-permute-done.6
  106.8 7.6 %conditional.13 = (f32[1,6,512]{2,1,0:T(8,128)S(1)}, f32[1,6,512,128]{2,3,1,0:T(8,128)}) conditional(s32[]{:T(128)} %bitcast.101, (f32[1,6,512]{2,1,0:T(8,128)S(1)}, f32[1,6,512,128]{3,2,1,0:T(8,128)S(1)}) %tuple.56, (bf16[2,512,128]{2,1,0:T(8,128)(2,1)S(1)}, bf16[512,1,6,128]{0,3,2,1:T(8,128)(2,1)S(1)}, f32[1,6,512]{2,1,0:T(8,128)S(1)}, ...), branch_computations={%region_26.0_spmd, %region_27.0_spmd} | conditional | flops 818688000 | bytes 26394640 | solution.py:73
  106.8 1.0 bitcast_reduce_fusion.6
  107.8 1.0 fusion.110
  108.9 2.5 bitcast_add_fusion.12
  111.4 3.0 %copy.47 = f32[1,6,512,128]{2,3,1,0:T(8,128)} copy(f32[1,6,512,128]{3,2,1,0:T(8,128)} %bitcast_add_fusion.12) | data formatting | bytes 3145728 | tf_op jit(solution)/shard_map/cond | solution.py:73
  114.5 1.6 divide_convert_fusion
  116.1 10.7 %convolution_convert_fusion = bf16[512,6144]{1,0:T(8,128)(2,1)} fusion(bf16[512,768]{0,1:T(8,128)(2,1)S(1)} %bitcast.406, bf16[768,6144]{1,0:T(8,128)(2,1)} %param.25), kind=kOutput, calls=%fused_computation.148 | convolution fusion | flops 4834983936 | bytes 16515072 | tf_op jit(solution)/shard_map/dot_general | solution.py:80
  126.8 0.0 reduce-scatter.2.cloned.1.call-update
  126.8 0.6 copy-done.14
  127.5 0.6 dynamic_slice.6
  128.0 1.0 fusion.140
  129.1 132.2 %reduce-scatter.2.cloned.1.call-done = bf16[64,6144]{1,0:T(8,128)(2,1)} async-done(((bf16[512,6144]{1,0:T(8,128)(2,1)}), bf16[64,6144]{1,0:T(8,128)(2,1)}) %reduce-scatter.2.cloned.1.call-update) | async-done | bytes 786448 | tf_op jit(solution)/shard_map/reduce_scatter | solution.py:79
  261.2 2.2 add_convert_fusion
  (45 shorter events, 0.3 us)
Async XLA Ops:
  6.5 121.5 %copy-start = (f32[32,6144]{1,0:T(8,128)S(1)}, f32[32,6144]{1,0:T(8,128)}, u32[]{:S(2)}) copy-start(f32[32,6144]{1,0:T(8,128)} %param.27) | copy-start | bytes 2359300
  6.5 53.5 %copy-start.2 = (bf16[512,128]{1,0:T(8,128)(2,1)S(1)}, bf16[512,128]{1,0:T(8,128)(2,1)}, u32[]{:S(2)}) copy-start(bf16[512,128]{1,0:T(8,128)(2,1)} %param.24) | copy-start | bytes 393220
  6.5 254.7 %reduce-scatter.2.cloned.1.call-start = ((), (), s32[]{:S(2)}) async-start(), calls=%async_computation.1 | async-start | bytes 7077888 | tf_op jit(solution)/shard_map/reduce_scatter | solution.py:79
  7.6 10.1 %collective-permute-start = (bf16[2,512,128]{2,1,0:T(8,128)(2,1)S(1)}, bf16[2,512,128]{2,1,0:T(8,128)(2,1)S(1)}, u32[]{:S(2)}, u32[]{:S(2)}) collective-permute-start(bf16[2,512,128]{2,1,0:T(8,128)(2,1)S(1)} %pad_maximum_fusion), channel_id=1, source_target_pairs={{0,8},{8,16},{16,24},{24,32},{32,40},{40,48},{48,56},{56,64},{64,7... | collective-permute-start | bytes 786440 | tf_op jit(solution)/shard_map/ppermute | solution.py:15
  17.7 42.3 %copy-start.11 = (bf16[2,512,128]{2,1,0:T(8,128)(2,1)}, bf16[2,512,128]{2,1,0:T(8,128)(2,1)S(1)}, u32[]{:S(2)}) copy-start(bf16[2,512,128]{2,1,0:T(8,128)(2,1)S(1)} %collective-permute-done) | copy-start | bytes 786436
  17.7 10.1 %collective-permute-start.1 = (bf16[2,512,128]{2,1,0:T(8,128)(2,1)S(1)}, bf16[2,512,128]{2,1,0:T(8,128)(2,1)S(1)}, u32[]{:S(2)}, u32[]{:S(2)}) collective-permute-start(bf16[2,512,128]{2,1,0:T(8,128)(2,1)S(1)} %collective-permute-done), channel_id=1, source_target_pairs={{0,8},{8,16},{16,24},{24,32},{32,40},{40,48},{48,56},{56,64},{64,7... | collective-permute-start | bytes 786440 | tf_op jit(solution)/shard_map/ppermute | solution.py:15
  27.8 32.2 %copy-start.9 = (bf16[2,512,128]{2,1,0:T(8,128)(2,1)}, bf16[2,512,128]{2,1,0:T(8,128)(2,1)S(1)}, u32[]{:S(2)}) copy-start(bf16[2,512,128]{2,1,0:T(8,128)(2,1)S(1)} %collective-permute-done.1) | copy-start | bytes 786436
  27.8 10.1 %collective-permute-start.2 = (bf16[2,512,128]{2,1,0:T(8,128)(2,1)S(1)}, bf16[2,512,128]{2,1,0:T(8,128)(2,1)S(1)}, u32[]{:S(2)}, u32[]{:S(2)}) collective-permute-start(bf16[2,512,128]{2,1,0:T(8,128)(2,1)S(1)} %collective-permute-done.1), channel_id=1, source_target_pairs={{0,8},{8,16},{16,24},{24,32},{32,40},{40,48},{48,56},{56,64},{64,7... | collective-permute-start | bytes 786440 | tf_op jit(solution)/shard_map/ppermute | solution.py:15
  37.9 22.1 %copy-start.7 = (bf16[2,512,128]{2,1,0:T(8,128)(2,1)}, bf16[2,512,128]{2,1,0:T(8,128)(2,1)S(1)}, u32[]{:S(2)}) copy-start(bf16[2,512,128]{2,1,0:T(8,128)(2,1)S(1)} %collective-permute-done.2) | copy-start | bytes 786436
  37.9 10.1 %collective-permute-start.3 = (bf16[2,512,128]{2,1,0:T(8,128)(2,1)S(1)}, bf16[2,512,128]{2,1,0:T(8,128)(2,1)S(1)}, u32[]{:S(2)}, u32[]{:S(2)}) collective-permute-start(bf16[2,512,128]{2,1,0:T(8,128)(2,1)S(1)} %collective-permute-done.2), channel_id=1, source_target_pairs={{0,8},{8,16},{16,24},{24,32},{32,40},{40,48},{48,56},{56,64},{64,7... | collective-permute-start | bytes 786440 | tf_op jit(solution)/shard_map/ppermute | solution.py:15
  48.0 12.0 %copy-start.5 = (bf16[2,512,128]{2,1,0:T(8,128)(2,1)}, bf16[2,512,128]{2,1,0:T(8,128)(2,1)S(1)}, u32[]{:S(2)}) copy-start(bf16[2,512,128]{2,1,0:T(8,128)(2,1)S(1)} %collective-permute-done.3) | copy-start | bytes 786436
  48.0 10.1 %collective-permute-start.4 = (bf16[2,512,128]{2,1,0:T(8,128)(2,1)S(1)}, bf16[2,512,128]{2,1,0:T(8,128)(2,1)S(1)}, u32[]{:S(2)}, u32[]{:S(2)}) collective-permute-start(bf16[2,512,128]{2,1,0:T(8,128)(2,1)S(1)} %collective-permute-done.3), channel_id=1, source_target_pairs={{0,8},{8,16},{16,24},{24,32},{32,40},{40,48},{48,56},{56,64},{64,7... | collective-permute-start | bytes 786440 | tf_op jit(solution)/shard_map/ppermute | solution.py:15
  58.1 3.7 %copy-start.3 = (bf16[2,512,128]{2,1,0:T(8,128)(2,1)}, bf16[2,512,128]{2,1,0:T(8,128)(2,1)S(1)}, u32[]{:S(2)}) copy-start(bf16[2,512,128]{2,1,0:T(8,128)(2,1)S(1)} %collective-permute-done.4) | copy-start | bytes 786436
  58.1 10.2 %collective-permute-start.5 = (bf16[2,512,128]{2,1,0:T(8,128)(2,1)S(1)}, bf16[2,512,128]{2,1,0:T(8,128)(2,1)}, u32[]{:S(2)}, u32[]{:S(2)}) collective-permute-start(bf16[2,512,128]{2,1,0:T(8,128)(2,1)S(1)} %collective-permute-done.4), channel_id=1, source_target_pairs={{0,8},{8,16},{16,24},{24,32},{32,40},{40,48},{48,56},{56,64},{64,7... | collective-permute-start | bytes 786440 | tf_op jit(solution)/shard_map/ppermute | solution.py:15
  60.0 11.2 %copy-start.13 = (s32[32]{0:T(128)S(1)}, s32[32]{0:T(128)}, u32[]{:S(2)}) copy-start(s32[32]{0:T(128)} %param.29) | copy-start | bytes 388
  68.3 38.6 %collective-permute-start.6 = (bf16[2,512,128]{2,1,0:T(8,128)(2,1)}, bf16[2,512,128]{2,1,0:T(8,128)(2,1)S(1)}, u32[]{:S(2)}, u32[]{:S(2)}) collective-permute-start(bf16[2,512,128]{2,1,0:T(8,128)(2,1)} %collective-permute-done.5), channel_id=1, source_target_pairs={{0,8},{8,16},{16,24},{24,32},{32,40},{40,48},{48,56},{56,64},{64,7... | collective-permute-start | bytes 786440 | tf_op jit(solution)/shard_map/ppermute | solution.py:15
  76.3 3.1 %copy-start.12 = (bf16[2,512,128]{2,1,0:T(8,128)(2,1)S(1)}, bf16[2,512,128]{2,1,0:T(8,128)(2,1)}, u32[]{:S(2)}) copy-start(bf16[2,512,128]{2,1,0:T(8,128)(2,1)} %get-tuple-element.116) | copy-start | bytes 786436 | tf_op jit(solution)/shard_map/cond
  81.2 3.1 %copy-start.10 = (bf16[2,512,128]{2,1,0:T(8,128)(2,1)S(1)}, bf16[2,512,128]{2,1,0:T(8,128)(2,1)}, u32[]{:S(2)}) copy-start(bf16[2,512,128]{2,1,0:T(8,128)(2,1)} %get-tuple-element.121) | copy-start | bytes 786436 | tf_op jit(solution)/shard_map/cond
  86.2 3.0 %copy-start.8 = (bf16[2,512,128]{2,1,0:T(8,128)(2,1)S(1)}, bf16[2,512,128]{2,1,0:T(8,128)(2,1)}, u32[]{:S(2)}) copy-start(bf16[2,512,128]{2,1,0:T(8,128)(2,1)} %get-tuple-element.126) | copy-start | bytes 786436 | tf_op jit(solution)/shard_map/cond
  91.1 3.1 %copy-start.6 = (bf16[2,512,128]{2,1,0:T(8,128)(2,1)S(1)}, bf16[2,512,128]{2,1,0:T(8,128)(2,1)}, u32[]{:S(2)}) copy-start(bf16[2,512,128]{2,1,0:T(8,128)(2,1)} %get-tuple-element.131) | copy-start | bytes 786436 | tf_op jit(solution)/shard_map/cond
  96.0 3.1 %copy-start.4 = (bf16[2,512,128]{2,1,0:T(8,128)(2,1)S(1)}, bf16[2,512,128]{2,1,0:T(8,128)(2,1)}, u32[]{:S(2)}) copy-start(bf16[2,512,128]{2,1,0:T(8,128)(2,1)} %get-tuple-element.136) | copy-start | bytes 786436 | tf_op jit(solution)/shard_map/cond
  126.8 0.7 copy-start.14
  126.8 134.4 %copy-start.1 = (bf16[64,6144]{1,0:T(8,128)(2,1)S(1)}, bf16[64,6144]{1,0:T(8,128)(2,1)}, u32[]{:S(2)}) copy-start(bf16[64,6144]{1,0:T(8,128)(2,1)} %param.26) | copy-start | bytes 2359300
Sparse Core Ops, SparseCore 0:
  126.9 134.2 reduce-scatter.1
where the time goes:
time: 272 us; the launch traced here: 270 us
  waiting for transfers between devices  176 us (65%)
  matrix products  42.1 us (15%)
  between operations  18 us (7%)
  other arithmetic  13.5 us (5%)
  starting transfers between devices  13.4 us (5%)
  local copies, waits for them, and re-layouts  6.39 us (2%)
    reduce_scatter x1, waiting for transfers between devices, on_device(): lax.psum_scatter(jnp.dot(attention, out_weight, preferred_element_type=jn...  132 us
    ppermute x7, waiting for transfers between devices, shifted(): return lax.ppermute(block, axis, route)  44 us
    dot_general x8, matrix products, update(): jnp.einsum('grtu,ugd->grtd', weights.astype(jnp.bfloat16), value_row_bloc...  15.9 us
    dot_general x8, matrix products, update(): jnp.einsum('tgrd,ugd->grtu', grouped, key_row_block, preferred_element_ty...  14.4 us
    ppermute x7, starting transfers between devices, shifted(): return lax.ppermute(block, axis, route)  13.4 us
    dot_general x1, matrix products, on_device(): jnp.dot(attention, out_weight, preferred_element_type=jnp.float32)  10.7 us
    reduce_sum x8, other arithmetic, update(): row_total = row_total * rescale + jnp.sum(weights, axis=-1)  8.33 us
  transfers between devices with their start and end apart: 8, of which 7 were waited for; matrix products, arithmetic and copies ran while one was open for 14% of the time, Pallas kernels for 0%

commit v1 on v0

v1 whole, which is shorter than its diff:
```python
import math

import jax
import jax.numpy as jnp
from jax import lax
from jax.experimental import pallas as pl
from jax.experimental.pallas import tpu as pltpu
from jax.sharding import PartitionSpec as P

MESH = pl.DeviceIdType.MESH
HEAD_SIZE = 128
BLOCKS = 8
TQ = 256
NEG = -1e30
NPAIR = 6
CX = 512
CY = 512
X_RING = 4


def kernel(
    q_hbm,
    k_hbm,
    v_hbm,
    w_hbm,
    res_hbm,
    gate_hbm,
    noise_ref,
    older_ref,
    out_ref,
    kv,
    vx,
    qv,
    wv,
    resv,
    gatev,
    m_ref,
    acc,
    att,
    px,
    rx1,
    rx2,
    sx,
    hx,
    rx3,
    py,
    ry1,
    ry2,
    ry3,
    loc_sem,
    kv_send,
    kv_recv,
    rs_send,
    rs_recv,
):
    spans = lax.axis_size("span")
    planes = spans // 4
    r = lax.axis_index("span")
    z = r // 4
    pos = r % 4
    yh = pos // 2
    c = pos % 2
    h = lax.axis_index("head")
    x = h // 2
    yl = h % 2
    xr = (x + 1) % X_RING
    xl = (x + X_RING - 1) % X_RING
    xo = (x + 2) % X_RING
    right = xr * 2 + yl
    left = xl * 2 + yl
    ypair = x * 2 + (1 - yl)
    mate = r + 1 - 2 * c
    ymate = r + 2 - 4 * yh
    heads = qv.shape[1] // HEAD_SIZE
    rows = qv.shape[0]

    def local(src, dst, index):
        return pltpu.make_async_copy(src, dst, loc_sem.at[index])

    loads = [
        local(k_hbm, kv.at[0, 0], 0),
        local(v_hbm, kv.at[0, 1], 1),
        local(q_hbm, qv, 2),
        local(w_hbm, wv, 3),
        local(res_hbm, resv, 4),
        local(gate_hbm, gatev, 5),
    ]
    for load in loads:
        load.start()

    barrier = pltpu.get_barrier_semaphore()

    def greet(device):
        pl.semaphore_signal(barrier, inc=1, device_id=device, device_id_type=MESH)

    greet({"span": mate})
    greet({"span": ymate})
    greet({"head": right})
    greet({"head": left})
    greet({"head": ypair})

    @pl.when(z < planes - 1)
    def _():
        greet({"span": r + 4})

    @pl.when(z > 0)
    def _():
        greet({"span": r - 4})

    vx[:, HEAD_SIZE:] = jnp.ones((rows, HEAD_SIZE), jnp.bfloat16)
    m_ref[...] = jnp.full(m_ref.shape, NEG, jnp.float32)
    acc[...] = jnp.zeros(acc.shape, jnp.float32)
    full = 5 + jnp.where(z < planes - 1, 1, 0) + jnp.where(z > 0, 1, 0)
    pl.semaphore_wait(barrier, full)

    def kv_copy(index, source, target, span):
        return pltpu.make_async_remote_copy(
            src_ref=kv.at[source],
            dst_ref=kv.at[target],
            send_sem=kv_send.at[index],
            recv_sem=kv_recv.at[target],
            device_id={"span": span},
            device_id_type=MESH,
        )

    up = z < planes - 1
    routes = [
        (0, up, kv_copy(0, 0, 4, r + 4)),
        (0, yh == 0, kv_copy(1, 0, 2, ymate)),
        (0, c == 0, kv_copy(2, 0, 1, mate)),
        (4, yh == 1, kv_copy(3, 4, 2, ymate)),
        (4, c >= 0, kv_copy(4, 4, 5 - 2 * c, mate)),
        (2, up, kv_copy(5, 2, 6, r + 4)),
        (2, c >= 0, kv_copy(6, 2, 3 - 2 * c, mate)),
        (3, jnp.logical_and(up, c == 0), kv_copy(7, 3, 7, r + 4)),
        (6, c >= 0, kv_copy(8, 6, 7 - 2 * c, mate)),
    ]

    loads[0].wait()
    loads[1].wait()

    def forward(slot_static):
        for source, condition, copy in routes:
            if source == slot_static:

                @pl.when(condition)
                def _(copy=copy):
                    copy.start()

    forward(0)
    loads[2].wait()

    older = older_ref[r]
    scale = math.log2(math.e) / math.sqrt(HEAD_SIZE)
    units = [(g, t) for g in range(heads) for t in range(rows // TQ)]

    def attend(slot):
        seen = slot <= older
        vx[:, :HEAD_SIZE] = kv[slot, 1]
        keys = kv[slot, 0]

        def score(unit):
            g, t = unit
            return lax.dot_general(
                qv[t * TQ : (t + 1) * TQ, g * HEAD_SIZE : (g + 1) * HEAD_SIZE],
                keys,
                (((1,), (1,)), ((), ())),
                preferred_element_type=jnp.float32,
            )

        ahead = score(units[0])
        for index, (g, t) in enumerate(units):
            s = ahead
            if index + 1 < len(units):
                ahead = score(units[index + 1])
            part = slice(t * TQ, (t + 1) * TQ)
            before = m_ref[g, part]
            top = jnp.max(s, axis=1, keepdims=True) * scale
            top = jnp.where(seen, top, NEG)
            now = jnp.maximum(before, top)
            m_ref[g, part] = now
            base = jnp.where(seen, now, -NEG)
            p = jnp.exp2(s * scale - jnp.tile(base, (1, s.shape[1] // 128)))
            alpha = jnp.exp2(before - now)
            added = jnp.dot(
                p.astype(jnp.bfloat16), vx[...], preferred_element_type=jnp.float32
            )
            acc[g, part] = acc[g, part] * jnp.tile(alpha, (1, 2)) + added

    def arrive(j, carry):
        slot0 = jnp.where(j == 0, 0, jnp.where(j < 5, 5 - j, 12 - j))
        slot1 = jnp.where(
            j == 1, 1, jnp.where(jnp.logical_or(j == 2, j == 3), j + 2, jnp.where(
                jnp.logical_or(j == 4, j == 5), j - 2, j))
        )
        slot = jnp.where(c == 0, slot0, slot1)

        @pl.when(r >= slot)
        def _():
            @pl.when(slot > 0)
            def _():
                pltpu.make_async_copy(
                    kv.at[slot], kv.at[slot], kv_recv.at[slot]
                ).wait()

            for s in (4, 2, 3, 6):

                @pl.when(slot == s)
                def _(s=s):
                    forward(s)

            attend(slot)

        return carry

    lax.fori_loop(0, BLOCKS, arrive, 0)

    for g in range(heads):
        att[:, g * HEAD_SIZE : (g + 1) * HEAD_SIZE] = (
            acc[g, :, :HEAD_SIZE] / acc[g, :, HEAD_SIZE:]
        ).astype(jnp.bfloat16)

    for load in loads[3:]:
        load.wait()

    step = noise_ref[r]

    def rs_copy(i, index, source, target, device):
        return pltpu.make_async_remote_copy(
            src_ref=source,
            dst_ref=target,
            send_sem=rs_send.at[i, index],
            recv_sem=rs_recv.at[i, index],
            device_id={"head": device},
            device_id_type=MESH,
        )

    def x1(i):
        return (
            rs_copy(i, 0, px.at[i, xo, pl.ds(0, 64)], rx1.at[i, 0], right),
            rs_copy(i, 1, px.at[i, xo, pl.ds(64, 64)], rx1.at[i, 1], left),
        )

    def x2(i):
        return (
            rs_copy(i, 2, px.at[i, xr], rx2.at[i, 0], right),
            rs_copy(i, 3, px.at[i, xl], rx2.at[i, 1], left),
        )

    def x3(i):
        return (rs_copy(i, 4, sx.at[i], rx3.at[i], ypair),)

    def y1(i):
        return (rs_copy(i, 5, py.at[i, 1 - yl], ry1.at[i], ypair),)

    def y2(i):
        return (
            rs_copy(i, 6, py.at[i, yl, xo, pl.ds(0, 32)], ry2.at[i, 0], right),
            rs_copy(i, 7, py.at[i, yl, xo, pl.ds(32, 32)], ry2.at[i, 1], left),
        )

    def y3(i):
        return (
            rs_copy(i, 8, py.at[i, yl, xr], ry3.at[i, 0], right),
            rs_copy(i, 9, py.at[i, yl, xl], ry3.at[i, 1], left),
        )

    def start(copies):
        for copy in copies:
            copy.start()

    def landed(copies):
        for copy in copies:
            copy.wait_recv()

    def f32(value):
        return value.astype(jnp.float32)

    def bf16(value):
        return value.astype(jnp.bfloat16)

    def finish(first, width, total):
        columns = pl.ds(pl.multiple_of(first, 128), width)
        gate = gatev[pl.ds(step, 1), columns]
        out_ref[:, columns] = bf16(f32(resv[:, columns]) + gate * total)

    def stage(s, carry):
        @pl.when(s < NPAIR)
        def _():
            i = s
            first = pl.multiple_of(i * (CX + CY), 128)
            wide = jnp.dot(
                att[...], wv[:, pl.ds(first, CX)], preferred_element_type=jnp.float32
            )
            px[i] = bf16(wide).reshape(X_RING, 128, CX)
            start(x1(i))
            second = pl.multiple_of(first + CX, 128)
            wide = jnp.dot(
                att[...], wv[:, pl.ds(second, CY)], preferred_element_type=jnp.float32
            )
            wide = bf16(wide).reshape(X_RING, 2, 64, CY)
            py[i, 0] = wide[:, 0]
            py[i, 1] = wide[:, 1]
            start(y1(i))

        @pl.when(jnp.logical_and(s >= 1, s < NPAIR + 1))
        def _():
            i = s - 1
            landed(x1(i))
            px[i, xr, pl.ds(0, 64)] = bf16(f32(px[i, xr, pl.ds(0, 64)]) + f32(rx1[i, 0]))
            px[i, xl, pl.ds(64, 64)] = bf16(
                f32(px[i, xl, pl.ds(64, 64)]) + f32(rx1[i, 1])
            )
            start(x2(i))
            landed(y1(i))
            py[i, yl] = bf16(f32(py[i, yl]) + f32(ry1[i]))
            start(y2(i))

        @pl.when(jnp.logical_and(s >= 2, s < NPAIR + 2))
        def _():
            i = s - 2
            landed(x2(i))
            away = pl.ds(pl.multiple_of((1 - yl) * 64, 64), 64)
            mine = pl.ds(pl.multiple_of(yl * 64, 64), 64)
            sx[i] = bf16(
                f32(px[i, x, away]) + f32(rx2[i, 0, away]) + f32(rx2[i, 1, away])
            )
            start(x3(i))
            hx[i] = f32(px[i, x, mine]) + f32(rx2[i, 0, mine]) + f32(rx2[i, 1, mine])
            landed(y2(i))
            py[i, yl, xr, pl.ds(0, 32)] = bf16(
                f32(py[i, yl, xr, pl.ds(0, 32)]) + f32(ry2[i, 0])
            )
            py[i, yl, xl, pl.ds(32, 32)] = bf16(
                f32(py[i, yl, xl, pl.ds(32, 32)]) + f32(ry2[i, 1])
            )
            start(y3(i))

        @pl.when(s >= 3)
        def _():
            i = s - 3
            landed(x3(i))
            finish(i * (CX + CY), CX, hx[i] + f32(rx3[i]))
            landed(y3(i))
            total = f32(py[i, yl, x]) + f32(ry3[i, 0]) + f32(ry3[i, 1])
            finish(i * (CX + CY) + CX, CY, total)

        return carry

    lax.fori_loop(0, NPAIR + 3, stage, 0)

    for source, condition, copy in routes:

        @pl.when(jnp.logical_and(condition, r >= source))
        def _(copy=copy):
            copy.wait_send()

    def drain(i, carry):
        for copies in (x1(i), x2(i), x3(i), y1(i), y2(i), y3(i)):
            for copy in copies:
                copy.wait_send()
        return carry

    lax.fori_loop(0, NPAIR, drain, 0)


def on_device(q, k, v, w, residual, gate_table, noise_step, older_count):
    rows, width = q.shape
    heads = width // HEAD_SIZE
    any_space = pl.BlockSpec(memory_space=pl.ANY)
    smem = pl.BlockSpec(memory_space=pltpu.SMEM)
    bf, f3 = jnp.bfloat16, jnp.float32
    flops = 2 * rows * width * (w.shape[1] + 2 * BLOCKS * rows)
    return pl.pallas_call(
        kernel,
        out_shape=jax.ShapeDtypeStruct(residual.shape, residual.dtype),
        in_specs=[any_space] * 6 + [smem] * 2,
        out_specs=pl.BlockSpec(memory_space=pltpu.VMEM),
        scratch_shapes=[
            pltpu.VMEM((BLOCKS, 2, rows, HEAD_SIZE), bf),
            pltpu.VMEM((rows, 2 * HEAD_SIZE), bf),
            pltpu.VMEM((rows, width), bf),
            pltpu.VMEM(w.shape, bf),
            pltpu.VMEM(residual.shape, bf),
            pltpu.VMEM(gate_table.shape, f3),
            pltpu.VMEM((heads, rows, 128), f3),
            pltpu.VMEM((heads, rows, 2 * HEAD_SIZE), f3),
            pltpu.VMEM((rows, width), bf),
            pltpu.VMEM((NPAIR, X_RING, 128, CX), bf),
            pltpu.VMEM((NPAIR, 2, 64, CX), bf),
            pltpu.VMEM((NPAIR, 2, 128, CX), bf),
            pltpu.VMEM((NPAIR, 64, CX), bf),
            pltpu.VMEM((NPAIR, 64, CX), f3),
            pltpu.VMEM((NPAIR, 64, CX), bf),
            pltpu.VMEM((NPAIR, 2, X_RING, 64, CY), bf),
            pltpu.VMEM((NPAIR, X_RING, 64, CY), bf),
            pltpu.VMEM((NPAIR, 2, 32, CY), bf),
            pltpu.VMEM((NPAIR, 2, 64, CY), bf),
            pltpu.SemaphoreType.DMA((6,)),
            pltpu.SemaphoreType.DMA((9,)),
            pltpu.SemaphoreType.DMA((BLOCKS,)),
            pltpu.SemaphoreType.DMA((NPAIR, 10)),
            pltpu.SemaphoreType.DMA((NPAIR, 10)),
        ],
        compiler_params=pltpu.CompilerParams(
            collective_id=0, has_side_effects=True, vmem_limit_bytes=60 * 1024 * 1024
        ),
        cost_estimate=pl.CostEstimate(
            flops=flops,
            bytes_accessed=2 * w.size,
            transcendentals=rows * BLOCKS * rows * heads,
        ),
    )(q, k, v, w, residual, gate_table, noise_step, older_count)


def solution(mesh):
    in_specs = (
        P("span", "head"),
        P("span", "head"),
        P("span", "head"),
        P("head", None),
        P(("span", "head"), None),
        P(),
        P(),
        P(),
    )
    out_specs = P(("span", "head"), None)
    return jax.shard_map(
        on_device, mesh=mesh, in_specs=in_specs, out_specs=out_specs, check_vma=False
    )
```

time: 272 us -> 85.4 us (0.31)
  waiting for transfers between devices: 176 us -> 0 us
  Pallas kernels: 0 us -> 82.8 us
  matrix products: 42.1 us -> 0 us
  between operations: 18 us -> 0.01 us
  other arithmetic: 13.5 us -> 0 us
  starting transfers between devices: 13.4 us -> 0 us
  local copies, waits for them, and re-layouts: 6.39 us -> 2.06 us
    reduce_scatter x1 -> x0, waiting for transfers between devices: 132 us -> none  [on_device(): lax.psum_scatter(jnp.dot(attention, out_weight, preferred_element_type=jn...]
    pallas_call x0 -> x1, Pallas kernels: none -> 82.8 us  [on_device(): pl.pallas_call(kernel, out_shape=jax.ShapeDtypeStruct(residual.shape, res...]
    ppermute x7 -> x0, waiting for transfers between devices: 44 us -> none  [shifted(): return lax.ppermute(block, axis, route)]
    dot_general x18 -> x0, matrix products: 42.1 us -> none  [the longest x8 15.9 us: update(): jnp.einsum('grtu,ugd->grtd', weights.astype(jnp.bfloat16), value_row_bloc...]
    ppermute x7 -> x0, starting transfers between devices: 13.4 us -> none  [shifted(): return lax.ppermute(block, axis, route)]
    reduce_sum x8 -> x0, other arithmetic: 8.33 us -> none  [update(): row_total = row_total * rescale + jnp.sum(weights, axis=-1)]
    convert_element_type x2 -> x0, other arithmetic: 3.85 us -> none  [the longest x1 2.24 us: on_device(): (residual.astype(jnp.float32) + gate_row * projected).astype(jnp.bfloat16)]
    cond x17 -> x0, local copies, waits for them, and re-layouts: 3.08 us -> none  [the longest x1 3.04 us: on_device(): lax.cond(visible, lambda current: update(current, guarded_kv_block), keep...]
  transfers between devices with their start and end apart: 8 -> 0, of which waited for: 7 -> 0; matrix products, arithmetic and copies ran while one was open for 14% -> 0% of each run, Pallas kernels for 0% -> 0%
where the time goes in v1:
time: 85.4 us; the launch traced here: 84.9 us
  Pallas kernels  82.8 us (97%)
  local copies, waits for them, and re-layouts  2.06 us (2%)
    pallas_call x1, Pallas kernels, on_device(): pl.pallas_call(kernel, out_shape=jax.ShapeDtypeStruct(residual.shape, res...  82.8 us
    unnamed x1, local copies, waits for them, and re-layouts  2.06 us

profile of v1, /device:TPU:160, one launch (start us, length us, event | category | flops | bytes accessed | tf_op | source)
XLA Modules:
  0.0 84.9 jit_solution(6622561950473074562)
XLA Ops:
  0.0 82.8 %shard_map.82 = bf16[64,6144]{1,0:T(8,128)(2,1)} custom-call(bf16[512,768]{1,0:T(8,128)(2,1)} %q_hbm.1, bf16[512,128]{1,0:T(8,128)(2,1)} %k_hbm.1, bf16[512,128]{1,0:T(8,128)(2,1)} %v_hbm.1, bf16[768,6144]{1,0:T(8,128)(2,1)} %w_hbm.1, bf16[64,6144]{1,0:T(8,128)(2,1)} %res_hbm.1, f32[32,6144]{1,0:T(8,128)} %gate_hbm.1, s32[32]{0:T(128)} %noise_ref.1, s32[32]{0:T(128)} %older_ref.1), custom_call_target="tpu_custom_call" | custom-call | flops 11274289152 | bytes 9437184 | tf_op jit(solution)/shard_map/pallas_call | solution.py:374
  82.8 2.1 %copy.10 = bf16[64,6144]{1,0:T(8,128)(2,1)} copy(bf16[64,6144]{1,0:T(8,128)(2,1)} %shard_map.82) | data formatting | bytes 1572864

commit v2 on v1

v2 whole, which is shorter than its diff:
```python
import math

import jax
import jax.numpy as jnp
from jax import lax
from jax.experimental import pallas as pl
from jax.experimental.pallas import tpu as pltpu
from jax.sharding import PartitionSpec as P

MESH = pl.DeviceIdType.MESH
HEAD_SIZE = 128
BLOCKS = 8
HALVES = 2
AT_ONCE = 3
NEG = -1e30
GROUPS = 6
UNITS = HALVES * GROUPS
CX = 512
CY = 512
LAG = 3
X_RING = 4


def kernel(
    q_hbm,
    k_hbm,
    v_hbm,
    w_hbm,
    res_hbm,
    gate_hbm,
    noise_ref,
    older_ref,
    out_ref,
    kv,
    vx,
    qv,
    wv,
    resv,
    gatev,
    m_ref,
    acc,
    att,
    px,
    rx1,
    rx2,
    sx,
    hx,
    rx3,
    py,
    ry1,
    ry2,
    ry3,
    loc_sem,
    kv_send,
    kv_recv,
    rs_send,
    rs_recv,
):
    spans = lax.axis_size("span")
    planes = spans // 4
    r = lax.axis_index("span")
    z = r // 4
    pos = r % 4
    yh = pos // 2
    c = pos % 2
    h = lax.axis_index("head")
    x = h // 2
    yl = h % 2
    xr = (x + 1) % X_RING
    xl = (x + X_RING - 1) % X_RING
    xo = (x + 2) % X_RING
    right = xr * 2 + yl
    left = xl * 2 + yl
    ypair = x * 2 + (1 - yl)
    mate = r + 1 - 2 * c
    ymate = r + 2 - 4 * yh
    rows = kv.shape[2]
    heads = qv.shape[3] // HEAD_SIZE
    half_rows = qv.shape[1] * qv.shape[2]
    piece = qv.shape[2]

    def local(src, dst, index):
        return pltpu.make_async_copy(src, dst, loc_sem.at[index])

    loads = [
        local(k_hbm, kv.at[0, 0], 0),
        local(v_hbm, kv.at[0, 1], 1),
        local(q_hbm.at[:, 0], qv.at[0], 2),
        local(q_hbm.at[:, 1], qv.at[1], 3),
        local(w_hbm, wv, 4),
        local(res_hbm, resv, 5),
        local(gate_hbm, gatev, 6),
    ]
    for load in loads:
        load.start()

    barrier = pltpu.get_barrier_semaphore()

    def greet(device):
        pl.semaphore_signal(barrier, inc=1, device_id=device, device_id_type=MESH)

    greet({"span": mate})
    greet({"span": ymate})
    greet({"head": right})
    greet({"head": left})
    greet({"head": ypair})

    @pl.when(z < planes - 1)
    def _():
        greet({"span": r + 4})

    @pl.when(z > 0)
    def _():
        greet({"span": r - 4})

    vx[:, HEAD_SIZE:] = jnp.ones((rows, HEAD_SIZE), jnp.bfloat16)
    m_ref[...] = jnp.full(m_ref.shape, NEG, jnp.float32)
    acc[...] = jnp.zeros(acc.shape, jnp.float32)
    full = 5 + jnp.where(z < planes - 1, 1, 0) + jnp.where(z > 0, 1, 0)
    pl.semaphore_wait(barrier, full)

    def kv_copy(index, part, source, target, span):
        return pltpu.make_async_remote_copy(
            src_ref=kv.at[source, part],
            dst_ref=kv.at[target, part],
            send_sem=kv_send.at[index, part],
            recv_sem=kv_recv.at[target, part],
            device_id={"span": span},
            device_id_type=MESH,
        )

    up = z < planes - 1
    always = c >= 0
    routes = [
        (0, up, 4, r + 4),
        (0, yh == 0, 2, ymate),
        (0, c == 0, 1, mate),
        (4, yh == 1, 2, ymate),
        (4, always, 5 - 2 * c, mate),
        (2, up, 6, r + 4),
        (2, always, 3 - 2 * c, mate),
        (3, jnp.logical_and(up, c == 0), 7, r + 4),
        (6, always, 7 - 2 * c, mate),
    ]

    def forward(arrived, part):
        for index, (source, condition, target, span) in enumerate(routes):
            if source == arrived:

                @pl.when(condition)
                def _(index=index, source=source, target=target, span=span):
                    kv_copy(index, part, source, target, span).start()

    for part in (0, 1):
        loads[part].wait()
        forward(0, part)
    loads[2].wait()
    loads[3].wait()

    older = older_ref[r]
    scale = math.log2(math.e) / math.sqrt(HEAD_SIZE)

    def attend(slot, half):
        seen = slot <= older
        vx[:, :HEAD_SIZE] = kv[slot, 1]
        keys = kv[slot, 0]

        def score(g):
            mine = qv[half, :, :, g * HEAD_SIZE : (g + 1) * HEAD_SIZE]
            return lax.dot_general(
                mine.reshape(half_rows, HEAD_SIZE),
                keys,
                (((1,), (1,)), ((), ())),
                preferred_element_type=jnp.float32,
            )

        ahead = score(0)
        for g in range(heads):
            s = ahead
            if g + 1 < heads:
                ahead = score(g + 1)
            before = m_ref[half, g]
            top = jnp.max(s, axis=1, keepdims=True) * scale
            top = jnp.where(seen, top, NEG)
            now = jnp.maximum(before, top)
            m_ref[half, g] = now
            base = jnp.where(seen, now, -NEG)
            p = jnp.exp2(s * scale - jnp.tile(base, (1, s.shape[1] // 128)))
            alpha = jnp.exp2(before - now)
            added = jnp.dot(
                p.astype(jnp.bfloat16), vx[...], preferred_element_type=jnp.float32
            )
            acc[half, g] = acc[half, g] * jnp.tile(alpha, (1, 2)) + added

    def packed(slots):
        return sum(slot * 8**place for place, slot in enumerate(slots))

    orders = ([0, 4, 3, 2, 1, 7, 6, 5], [0, 1, 4, 5, 2, 3, 6, 7])

    def pick(slots0, slots1):
        return jnp.where(c == 0, packed(slots0), packed(slots1))

    def landed_kv(slot, part):
        @pl.when(slot > 0)
        def _():
            pltpu.make_async_copy(
                kv.at[slot, part], kv.at[slot, part], kv_recv.at[slot, part]
            ).wait()

        for s in (4, 2, 3, 6):

            @pl.when(slot == s)
            def _(s=s):
                forward(s, part)

    def arrive(t, carry):
        left_over, previous = carry
        slot = left_over % 8
        there = r >= slot

        @pl.when(there)
        def _():
            landed_kv(slot, 0)

        fill = jnp.logical_and(t >= 1, t <= AT_ONCE)

        @pl.when(jnp.logical_and(fill, r >= previous))
        def _():
            attend(previous, 1)

        @pl.when(there)
        def _():
            landed_kv(slot, 1)
            attend(slot, 0)

        return left_over // 8, slot

    lax.fori_loop(0, BLOCKS, arrive, (pick(*orders), jnp.int32(0)))

    def settle(half):
        for g in range(heads):
            att[half, :, g * HEAD_SIZE : (g + 1) * HEAD_SIZE] = (
                acc[half, g, :, :HEAD_SIZE] / acc[half, g, :, HEAD_SIZE:]
            ).astype(jnp.bfloat16)

    settle(0)
    for load in loads[4:]:
        load.wait()

    step = noise_ref[r]

    def rs_copy(i, index, source, target, device):
        return pltpu.make_async_remote_copy(
            src_ref=source,
            dst_ref=target,
            send_sem=rs_send.at[i, index],
            recv_sem=rs_recv.at[i, index],
            device_id={"head": device},
            device_id_type=MESH,
        )

    def x1(i):
        return (
            rs_copy(i, 0, px.at[i, xo, pl.ds(0, piece)], rx1.at[i, 0], right),
            rs_copy(i, 1, px.at[i, xo, pl.ds(piece, piece)], rx1.at[i, 1], left),
        )

    def x2(i):
        return (
            rs_copy(i, 2, px.at[i, xr], rx2.at[i, 0], right),
            rs_copy(i, 3, px.at[i, xl], rx2.at[i, 1], left),
        )

    def x3(i):
        return (rs_copy(i, 4, sx.at[i], rx3.at[i], ypair),)

    def y1(i):
        return (rs_copy(i, 5, py.at[i, 1 - yl], ry1.at[i], ypair),)

    def y2(i):
        return (
            rs_copy(i, 6, py.at[i, yl, xo, pl.ds(0, piece // 2)], ry2.at[i, 0], right),
            rs_copy(i, 7, py.at[i, yl, xo, pl.ds(piece // 2, piece // 2)], ry2.at[i, 1], left),
        )

    def y3(i):
        return (
            rs_copy(i, 8, py.at[i, yl, xr], ry3.at[i, 0], right),
            rs_copy(i, 9, py.at[i, yl, xl], ry3.at[i, 1], left),
        )

    def start(copies):
        for copy in copies:
            copy.start()

    def landed(copies):
        for copy in copies:
            copy.wait_recv()

    def f32(value):
        return value.astype(jnp.float32)

    def bf16(value):
        return value.astype(jnp.bfloat16)

    def finish(i, shift, width, total):
        first = (i % GROUPS) * (CX + CY) + shift
        columns = pl.ds(pl.multiple_of(first, 128), width)
        mine = pl.ds(pl.multiple_of((i // GROUPS) * piece, piece), piece)
        gate = gatev[pl.ds(step, 1), columns]
        out_ref[mine, columns] = bf16(f32(resv[mine, columns]) + gate * total)

    low = pl.ds(0, piece)
    high = pl.ds(piece, piece)
    low2 = pl.ds(0, piece // 2)
    high2 = pl.ds(piece // 2, piece // 2)
    away = pl.ds(pl.multiple_of((1 - yl) * piece, piece), piece)
    kept = pl.ds(pl.multiple_of(yl * piece, piece), piece)

    def stage(s, later):
        slot = later % 8

        @pl.when(s < UNITS)
        def _():
            i = s
            half = i // GROUPS
            first = pl.multiple_of((i % GROUPS) * (CX + CY), 128)
            wide = jnp.dot(
                att[half], wv[:, pl.ds(first, CX)], preferred_element_type=jnp.float32
            )
            px[i] = bf16(wide).reshape(X_RING, 2 * piece, CX)
            start(x1(i))
            second = pl.multiple_of(first + CX, 128)
            wide = jnp.dot(
                att[half], wv[:, pl.ds(second, CY)], preferred_element_type=jnp.float32
            )
            wide = bf16(wide).reshape(X_RING, 2, piece, CY)
            py[i, 0] = wide[:, 0]
            py[i, 1] = wide[:, 1]
            start(y1(i))

        @pl.when(jnp.logical_and(s < BLOCKS - AT_ONCE, r >= slot))
        def _():
            attend(slot, 1)

        @pl.when(s == BLOCKS - AT_ONCE)
        def _():
            settle(1)

        @pl.when(jnp.logical_and(s >= LAG, s < UNITS + LAG))
        def _():
            i = s - LAG
            landed(x1(i))
            px[i, xr, low] = bf16(f32(px[i, xr, low]) + f32(rx1[i, 0]))
            px[i, xl, high] = bf16(f32(px[i, xl, high]) + f32(rx1[i, 1]))
            start(x2(i))
            landed(y1(i))
            py[i, yl] = bf16(f32(py[i, yl]) + f32(ry1[i]))
            start(y2(i))

        @pl.when(jnp.logical_and(s >= 2 * LAG, s < UNITS + 2 * LAG))
        def _():
            i = s - 2 * LAG
            landed(x2(i))
            sx[i] = bf16(
                f32(px[i, x, away]) + f32(rx2[i, 0, away]) + f32(rx2[i, 1, away])
            )
            start(x3(i))
            hx[i] = f32(px[i, x, kept]) + f32(rx2[i, 0, kept]) + f32(rx2[i, 1, kept])
            landed(y2(i))
            py[i, yl, xr, low2] = bf16(f32(py[i, yl, xr, low2]) + f32(ry2[i, 0]))
            py[i, yl, xl, high2] = bf16(f32(py[i, yl, xl, high2]) + f32(ry2[i, 1]))
            start(y3(i))

        @pl.when(s >= 3 * LAG)
        def _():
            i = s - 3 * LAG
            landed(x3(i))
            finish(i, 0, CX, hx[i] + f32(rx3[i]))
            landed(y3(i))
            total = f32(py[i, yl, x]) + f32(ry3[i, 0]) + f32(ry3[i, 1])
            finish(i, CX, CY, total)

        return later // 8

    lax.fori_loop(0, UNITS + 3 * LAG, stage, pick(orders[0][AT_ONCE:], orders[1][AT_ONCE:]))

    for index, (source, condition, target, span) in enumerate(routes):

        @pl.when(jnp.logical_and(condition, r >= source))
        def _(index=index, source=source, target=target, span=span):
            for part in (0, 1):
                kv_copy(index, part, source, target, span).wait_send()

    def drain(i, carry):
        for copies in (x1(i), x2(i), x3(i), y1(i), y2(i), y3(i)):
            for copy in copies:
                copy.wait_send()
        return carry

    lax.fori_loop(0, UNITS, drain, 0)


def on_device(q, k, v, w, residual, gate_table, noise_step, older_count):
    rows, width = q.shape
    heads = width // HEAD_SIZE
    half_rows = rows // HALVES
    piece = residual.shape[0] // HALVES
    q = q.reshape(half_rows // piece, HALVES, piece, width)
    any_space = pl.BlockSpec(memory_space=pl.ANY)
    smem = pl.BlockSpec(memory_space=pltpu.SMEM)
    bf, f3 = jnp.bfloat16, jnp.float32
    flops = 2 * rows * width * (w.shape[1] + 2 * BLOCKS * rows)
    return pl.pallas_call(
        kernel,
        out_shape=pltpu.VMEM(residual.shape, residual.dtype),
        in_specs=[any_space] * 6 + [smem] * 2,
        out_specs=pl.BlockSpec(memory_space=pltpu.VMEM),
        scratch_shapes=[
            pltpu.VMEM((BLOCKS, 2, rows, HEAD_SIZE), bf),
            pltpu.VMEM((rows, 2 * HEAD_SIZE), bf),
            pltpu.VMEM((HALVES, half_rows // piece, piece, width), bf),
            pltpu.VMEM(w.shape, bf),
            pltpu.VMEM(residual.shape, bf),
            pltpu.VMEM(gate_table.shape, f3),
            pltpu.VMEM((HALVES, heads, half_rows, 128), f3),
            pltpu.VMEM((HALVES, heads, half_rows, 2 * HEAD_SIZE), f3),
            pltpu.VMEM((HALVES, half_rows, width), bf),
            pltpu.VMEM((UNITS, X_RING, 2 * piece, CX), bf),
            pltpu.VMEM((UNITS, 2, piece, CX), bf),
            pltpu.VMEM((UNITS, 2, 2 * piece, CX), bf),
            pltpu.VMEM((UNITS, piece, CX), bf),
            pltpu.VMEM((UNITS, piece, CX), f3),
            pltpu.VMEM((UNITS, piece, CX), bf),
            pltpu.VMEM((UNITS, 2, X_RING, piece, CY), bf),
            pltpu.VMEM((UNITS, X_RING, piece, CY), bf),
            pltpu.VMEM((UNITS, 2, piece // 2, CY), bf),
            pltpu.VMEM((UNITS, 2, piece, CY), bf),
            pltpu.SemaphoreType.DMA((7,)),
            pltpu.SemaphoreType.DMA((9, 2)),
            pltpu.SemaphoreType.DMA((BLOCKS, 2)),
            pltpu.SemaphoreType.DMA((UNITS, 10)),
            pltpu.SemaphoreType.DMA((UNITS, 10)),
        ],
        compiler_params=pltpu.CompilerParams(
            collective_id=0, has_side_effects=True, vmem_limit_bytes=60 * 1024 * 1024
        ),
        cost_estimate=pl.CostEstimate(
            flops=flops,
            bytes_accessed=2 * w.size,
            transcendentals=rows * BLOCKS * rows * heads,
        ),
    )(q, k, v, w, residual, gate_table, noise_step, older_count)


def solution(mesh):
    in_specs = (
        P("span", "head"),
        P("span", "head"),
        P("span", "head"),
        P("head", None),
        P(("span", "head"), None),
        P(),
        P(),
        P(),
    )
    out_specs = P(("span", "head"), None)
    return jax.shard_map(
        on_device, mesh=mesh, in_specs=in_specs, out_specs=out_specs, check_vma=False
    )
```

time: 85.4 us -> 78.4 us (0.918)
  Pallas kernels: 82.8 us -> 76.9 us
  local copies, waits for them, and re-layouts: 2.06 us -> 0.88 us
    pallas_call x1, Pallas kernels: 82.8 us -> 76.9 us  [on_device(): pl.pallas_call(kernel, out_shape=pltpu.VMEM(residual.shape, residual.dtyp...]
    unnamed x1, local copies, waits for them, and re-layouts: 2.06 us -> 0.88 us
where the time goes in v2:
time: 78.4 us; the launch traced here: 77.8 us
  Pallas kernels  76.9 us (98%)
  local copies, waits for them, and re-layouts  0.88 us (1%)
    pallas_call x1, Pallas kernels, on_device(): pl.pallas_call(kernel, out_shape=pltpu.VMEM(residual.shape, residual.dtyp...  76.9 us

profile of v2, /device:TPU:160, one launch (start us, length us, event | category | flops | bytes accessed | tf_op | source)
XLA Modules:
  0.0 77.8 jit_solution(16979799028564011427)
XLA Ops:
  0.0 76.9 %shard_map.82 = bf16[64,6144]{1,0:T(8,128)(2,1)S(1)} custom-call(bf16[8,2,32,768]{3,2,1,0:T(8,128)(2,1)} %bitcast.1, bf16[512,128]{1,0:T(8,128)(2,1)} %k_hbm.1, bf16[512,128]{1,0:T(8,128)(2,1)} %v_hbm.1, bf16[768,6144]{1,0:T(8,128)(2,1)} %w_hbm.1, bf16[64,6144]{1,0:T(8,128)(2,1)} %res_hbm.1, f32[32,6144]{1,0:T(8,128)} %gate_hbm.1, s32[32]{0:T(128)} %noise_ref.1, ...), custom_call_target="tpu_custom_call" | custom-call | flops 11274289152 | bytes 9437184 | tf_op jit(solution)/shard_map/pallas_call | solution.py:414
  76.9 0.9 %copy.10 = bf16[64,6144]{1,0:T(8,128)(2,1)} copy(bf16[64,6144]{1,0:T(8,128)(2,1)S(1)} %shard_map.82) | data formatting | bytes 1572864

commit v3 on v2

--- a/solution.py
+++ b/solution.py
@@ -113,10 +113,20 @@
     def _():
         greet({"span": r - 4})
 
+    @pl.when(jnp.logical_and(c == 1, z < planes - 1))
+    def _():
+        greet({"span": r + 3})
+
+    @pl.when(jnp.logical_and(c == 0, z > 0))
+    def _():
+        greet({"span": r - 3})
+
     vx[:, HEAD_SIZE:] = jnp.ones((rows, HEAD_SIZE), jnp.bfloat16)
     m_ref[...] = jnp.full(m_ref.shape, NEG, jnp.float32)
     acc[...] = jnp.zeros(acc.shape, jnp.float32)
-    full = 5 + jnp.where(z < planes - 1, 1, 0) + jnp.where(z > 0, 1, 0)
+    above = jnp.where(z < planes - 1, 1, 0)
+    below = jnp.where(z > 0, 1, 0)
+    full = 5 + above + below + jnp.where(c == 1, above, below)
     pl.semaphore_wait(barrier, full)
 
     def kv_copy(index, part, source, target, span):
@@ -137,9 +147,9 @@
         (0, c == 0, 1, mate),
         (4, yh == 1, 2, ymate),
         (4, always, 5 - 2 * c, mate),
+        (4, jnp.logical_and(up, c == 1), 7, r + 3),
         (2, up, 6, r + 4),
         (2, always, 3 - 2 * c, mate),
-        (3, jnp.logical_and(up, c == 0), 7, r + 4),
         (6, always, 7 - 2 * c, mate),
     ]
 
@@ -195,7 +205,7 @@
     def packed(slots):
         return sum(slot * 8**place for place, slot in enumerate(slots))
 
-    orders = ([0, 4, 3, 2, 1, 7, 6, 5], [0, 1, 4, 5, 2, 3, 6, 7])
+    orders = ([0, 4, 3, 2, 7, 1, 6, 5], [0, 1, 4, 5, 2, 3, 6, 7])
 
     def pick(slots0, slots1):
         return jnp.where(c == 0, packed(slots0), packed(slots1))
@@ -207,7 +217,7 @@
                 kv.at[slot, part], kv.at[slot, part], kv_recv.at[slot, part]
             ).wait()
 
-        for s in (4, 2, 3, 6):
+        for s in (4, 2, 6):
 
             @pl.when(slot == s)
             def _(s=s):
@@ -325,11 +335,6 @@
             i = s
             half = i // GROUPS
             first = pl.multiple_of((i % GROUPS) * (CX + CY), 128)
-            wide = jnp.dot(
-                att[half], wv[:, pl.ds(first, CX)], preferred_element_type=jnp.float32
-            )
-            px[i] = bf16(wide).reshape(X_RING, 2 * piece, CX)
-            start(x1(i))
             second = pl.multiple_of(first + CX, 128)
             wide = jnp.dot(
                 att[half], wv[:, pl.ds(second, CY)], preferred_element_type=jnp.float32
@@ -338,6 +343,11 @@
             py[i, 0] = wide[:, 0]
             py[i, 1] = wide[:, 1]
             start(y1(i))
+            wide = jnp.dot(
+                att[half], wv[:, pl.ds(first, CX)], preferred_element_type=jnp.float32
+            )
+            px[i] = bf16(wide).reshape(X_RING, 2 * piece, CX)
+            start(x1(i))
 
         @pl.when(jnp.logical_and(s < BLOCKS - AT_ONCE, r >= slot))
         def _():

time: 78.4 us -> 77.5 us (0.989)
  no operation moved by 1% of the time
where the time goes in v3:
time: 77.5 us; the launch traced here: 77.4 us
  Pallas kernels  76.5 us (99%)
  local copies, waits for them, and re-layouts  0.88 us (1%)
    pallas_call x1, Pallas kernels, on_device(): pl.pallas_call(kernel, out_shape=pltpu.VMEM(residual.shape, residual.dtyp...  76.5 us

profile of v3, /device:TPU:160, one launch (start us, length us, event | category | flops | bytes accessed | tf_op | source)
XLA Modules:
  0.0 77.4 jit_solution(4385840874886701277)
XLA Ops:
  0.0 76.5 %shard_map.82 = bf16[64,6144]{1,0:T(8,128)(2,1)S(1)} custom-call(bf16[8,2,32,768]{3,2,1,0:T(8,128)(2,1)} %bitcast.1, bf16[512,128]{1,0:T(8,128)(2,1)} %k_hbm.1, bf16[512,128]{1,0:T(8,128)(2,1)} %v_hbm.1, bf16[768,6144]{1,0:T(8,128)(2,1)} %w_hbm.1, bf16[64,6144]{1,0:T(8,128)(2,1)} %res_hbm.1, f32[32,6144]{1,0:T(8,128)} %gate_hbm.1, s32[32]{0:T(128)} %noise_ref.1, ...), custom_call_target="tpu_custom_call" | custom-call | flops 11274289152 | bytes 9437184 | tf_op jit(solution)/shard_map/pallas_call | solution.py:424
  76.5 0.9 %copy.10 = bf16[64,6144]{1,0:T(8,128)(2,1)} copy(bf16[64,6144]{1,0:T(8,128)(2,1)S(1)} %shard_map.82) | data formatting | bytes 1572864

commit v4 on v3

--- a/solution.py
+++ b/solution.py
@@ -15,8 +15,8 @@
 NEG = -1e30
 GROUPS = 6
 UNITS = HALVES * GROUPS
-CX = 512
-CY = 512
+CX = 640
+CY = 384
 LAG = 3
 X_RING = 4
 

time: 77.5 us -> 81 us (1.045)
  Pallas kernels: 76.5 us -> 80.1 us
    pallas_call x1, Pallas kernels: 76.5 us -> 80.1 us  [on_device(): pl.pallas_call(kernel, out_shape=pltpu.VMEM(residual.shape, residual.dtyp...]
where the time goes in v4:
time: 81 us
  Pallas kernels  80.1 us (99%)
  local copies, waits for them, and re-layouts  0.88 us (1%)
    pallas_call x1, Pallas kernels, on_device(): pl.pallas_call(kernel, out_shape=pltpu.VMEM(residual.shape, residual.dtyp...  80.1 us

profile of v4, /device:TPU:160, one launch (start us, length us, event | category | flops | bytes accessed | tf_op | source)
XLA Modules:
  0.0 81.0 jit_solution(7313696805384763555)
XLA Ops:
  0.0 80.1 %shard_map.82 = bf16[64,6144]{1,0:T(8,128)(2,1)S(1)} custom-call(bf16[8,2,32,768]{3,2,1,0:T(8,128)(2,1)} %bitcast.1, bf16[512,128]{1,0:T(8,128)(2,1)} %k_hbm.1, bf16[512,128]{1,0:T(8,128)(2,1)} %v_hbm.1, bf16[768,6144]{1,0:T(8,128)(2,1)} %w_hbm.1, bf16[64,6144]{1,0:T(8,128)(2,1)} %res_hbm.1, f32[32,6144]{1,0:T(8,128)} %gate_hbm.1, s32[32]{0:T(128)} %noise_ref.1, ...), custom_call_target="tpu_custom_call" | custom-call | flops 11274289152 | bytes 9437184 | tf_op jit(solution)/shard_map/pallas_call | solution.py:424
  80.1 0.9 %copy.10 = bf16[64,6144]{1,0:T(8,128)(2,1)} copy(bf16[64,6144]{1,0:T(8,128)(2,1)S(1)} %shard_map.82) | data formatting | bytes 1572864
